TPU v7x, 512 devices: a whole 4x4x16 slice. The times are simulated.
512 devices in a mesh: snap: 16 (over y, x), plane: 32 (over z, core).
Axes of the slice: x: 4, y: 4, z: 16, core: 2. Of those that a mesh axis runs over, the one named last changes fastest.
Arguments:
- velocity: bfloat16 [16, 128, 3, 128, 128], P('snap', 'plane'), may hold values from -6 to 6
- plane_count: int32 [32], P('plane'), may hold values from 1 to 4, as said below
- inv_span: float32 [32, 4], P('plane'), may hold values from 0.5 to 4
- kernels: float32 [3, 2, 3, 3], replicated, may hold values from -2.4 to 2.4
- omega_block: int32 [32, 4], P('plane'), may hold values from 0 to 7
- omega_table: bfloat16 [8, 9, 32, 256], replicated, may hold values from -0.0625 to 0.0625
- omega_stream: bfloat16 [32, 256], replicated, may hold values from -6 to 6
- wall_shear: bfloat16 [16, 2, 128, 128], P('snap', None, 'plane'), may hold values from -6 to 6
Outputs:
- sketch: float32 [2, 32, 32, 256], P(None, 'plane', 'snap')
- gram: float32 [256, 256], replicated
Inputs may be any that keep to these rules, and one draw needn't show every extreme that they name: `plane_count`: every index of plane holds 1 or more live slots, slots 0 onwards; some index holds 4.
All inputs are finite; a program needn't handle non-finite values.
Results may differ from a plain program's by a relative error of at most 0.0043.
Values may be sent and summed in bfloat16 or wider, within the bound.
No kernel may reach another device: no remote copies, remote signals or barrier semaphores. Data moves between devices by JAX's collectives and lax.ppermute only.
A program may use at most 64 MiB of HBM per device.

v0:
```python
import jax
import jax.numpy as jnp
from jax import lax
from jax.sharding import PartitionSpec as P

X = 128
ZW = 128


def shifted(value, axis, steps):
    count = lax.axis_size(axis)
    leading, last = (max(0, -steps), min(count, count - steps))
    return lax.ppermute(value, axis, [(source, source + steps) for source in range(leading, last)])


def in_plane(centre, kernels):
    snaps, comps, zw, xw = centre.shape
    field = centre.astype(jnp.float32)
    padded = jnp.pad(field, ((0, 0), (0, 0), (1, 1), (1, 1)))
    first = jnp.zeros_like(field)
    second = jnp.zeros_like(field)
    for row_a in range(3):
        for col_b in range(3):
            window = padded[:, :, row_a : row_a + zw, col_b : col_b + xw]
            first = first + kernels[:, 0, row_a, col_b][None, :, None, None] * window
            second = second + kernels[:, 1, row_a, col_b][None, :, None, None] * window
    return (first, second)


def features(centre, below, above, span, kernels):
    snaps, comps, zw, xw = centre.shape
    first, second = in_plane(centre, kernels)
    normal = (above.astype(jnp.float32) - below.astype(jnp.float32)) * span
    grads = jnp.stack([first, second, normal], axis=2).reshape(snaps, 9, zw, xw)
    filtered = grads.reshape(snaps, 9, zw // 4, 4, xw // 4, 4).mean(axis=(3, 5))
    return filtered.astype(jnp.bfloat16)


def per_device(
    velocity, plane_count, inv_span, kernels, omega_block, omega_table, omega_stream, wall_shear
):
    slots = velocity.shape[1]
    live_count = plane_count[0]
    coef = jnp.zeros((velocity.shape[0], omega_stream.shape[1]), jnp.float32)
    last_live = lax.dynamic_index_in_dim(velocity, live_count - 1, 1, keepdims=False)
    from_below = shifted(last_live, "plane", 1)
    from_above = shifted(velocity[:, 0], "plane", -1)
    for slot in range(slots):
        below = from_below if slot == 0 else velocity[:, slot - 1]
        if slot + 1 < slots:
            above = jnp.where(slot + 1 < live_count, velocity[:, slot + 1], from_above)
        else:
            above = from_above
        feats = features(velocity[:, slot], below, above, inv_span[0, slot], kernels)
        proj = jnp.einsum("sczx,xk->sczk", feats, omega_stream, preferred_element_type=jnp.float32)
        table = lax.dynamic_index_in_dim(
            omega_table, omega_block[0, slot], 0, keepdims=False
        ).astype(jnp.float32)
        term = jnp.einsum("sczk,czk->sk", proj, table, precision=lax.Precision.HIGHEST)
        coef = coef + jnp.where(slot < live_count, term, jnp.zeros_like(term))
    coef = lax.psum(coef, "plane")
    snaps, comps, zw, xw = wall_shear.shape
    shear_f = (
        wall_shear.astype(jnp.float32)
        .reshape(snaps, comps, zw // 4, 4, xw // 4, 4)
        .mean(axis=(3, 5))
    )
    partial_sketch = jnp.einsum("smzx,sk->mzxk", shear_f, coef, precision=lax.Precision.HIGHEST)
    sketch = lax.psum_scatter(partial_sketch, "snap", scatter_dimension=2, tiled=True)
    total_rows = 2 * (X // 4) * (ZW // 4)
    flat = sketch.reshape(-1, sketch.shape[-1])
    local_gram = jnp.dot(flat.T, flat, precision=lax.Precision.HIGHEST)
    gram = lax.psum(local_gram, ("snap", "plane")) / jnp.float32(total_rows)
    return (sketch, gram)


def solution(mesh):
    return jax.shard_map(
        per_device,
        mesh=mesh,
        in_specs=(
            P("snap", "plane", None, None, None),
            P("plane"),
            P("plane", None),
            P(),
            P("plane", None),
            P(),
            P(),
            P("snap", None, "plane", None),
        ),
        out_specs=(P(None, "plane", "snap", None), P()),
        check_vma=False,
    )
```

profile of v0, /device:TPU:2, one launch (start us, length us, event | category | flops | bytes accessed | tf_op | source)
XLA Modules:
  0.0 790.4 jit_solution(1391584907513652331)
XLA Ops:
  7.2 0.0 copy-start
  7.2 0.0 copy-start.5
  7.2 0.0 copy-start.3
  7.2 0.0 copy-start.7
  7.2 0.0 all-reduce.10.cloned.1.call-start
  7.9 1.2 fusion.21
  9.1 1.3 collective-permute-start
  10.4 3.0 collective-permute-start.1
  13.4 0.0 copy-done.5
  13.4 0.7 fusion.23
  19.2 0.0 copy-done.3
  19.2 0.2 slice_reduce_fusion.17
  19.5 0.0 copy-done.7
  19.5 0.1 reduce_sum.53
  19.6 0.1 reduce_sum.54
  22.2 1.3 add_bitcast_fusion.7
  23.6 0.0 copy-start.6
  23.6 0.0 copy-start.1
  23.6 1.3 add_bitcast_fusion.6
  24.9 0.0 copy-done.6
  24.9 0.7 fusion.22
  25.6 0.0 collective-permute-done
  25.6 0.0 collective-permute-done.1
  25.6 0.0 copy-done.1
  25.6 2.7 multiply_bitcast_fusion.3
  28.3 0.1 pad_maximum_fusion
  28.4 21.0 %reshape_reshape.12 = f32[9,32,4,32,4]{4,3,2,1,0:T(8,128)} reshape(f32[1,3,3,128,128]{4,3,2,1,0:T(8,128)S(1)} %copy.14) | data formatting | bytes 1179648 | tf_op jit(solution)/shard_map/reshape;reshape | solution.py:35
  49.5 7.9 %reduce_sum.55 = f32[9,32,32]{2,1,0:T(8,128)S(1)} reduce(f32[9,32,4,32,4]{4,3,2,1,0:T(8,128)} %reshape_reshape.12, f32[]{:T(128)} %constant.38.clone.1), dimensions={2,4}, to_apply=%region_2.3 | reduce | flops 138240 | bytes 626692 | tf_op jit(solution)/shard_map/reduce_sum | solution.py:35
  57.4 20.8 %reshape_reshape.13 = f32[9,32,4,32,4]{4,3,2,1,0:T(8,128)} reshape(f32[1,3,3,128,128]{4,3,2,1,0:T(8,128)S(1)} %copy.15) | data formatting | bytes 1179648 | tf_op jit(solution)/shard_map/reshape;reshape | solution.py:35
  78.3 7.9 %reduce_sum.56 = f32[9,32,32]{2,1,0:T(8,128)S(1)} reduce(f32[9,32,4,32,4]{4,3,2,1,0:T(8,128)} %reshape_reshape.13, f32[]{:T(128)} %constant.38.clone.1), dimensions={2,4}, to_apply=%region_3.4 | reduce | flops 138240 | bytes 626692 | tf_op jit(solution)/shard_map/reduce_sum | solution.py:35
  86.2 0.1 pad_maximum_fusion.2
  86.3 20.8 %reshape_reshape.14 = f32[9,32,4,32,4]{4,3,2,1,0:T(8,128)} reshape(f32[1,3,3,128,128]{4,3,2,1,0:T(8,128)S(1)} %copy.16) | data formatting | bytes 1179648 | tf_op jit(solution)/shard_map/reshape;reshape | solution.py:35
  107.2 7.9 %reduce_sum.57 = f32[9,32,32]{2,1,0:T(8,128)S(1)} reduce(f32[9,32,4,32,4]{4,3,2,1,0:T(8,128)} %reshape_reshape.14, f32[]{:T(128)} %constant.38.clone.1), dimensions={2,4}, to_apply=%region_4.5 | reduce | flops 138240 | bytes 626692 | tf_op jit(solution)/shard_map/reduce_sum | solution.py:35
  115.2 20.8 %reshape_reshape.15 = f32[9,32,4,32,4]{4,3,2,1,0:T(8,128)} reshape(f32[1,3,3,128,128]{4,3,2,1,0:T(8,128)S(1)} %copy.17) | data formatting | bytes 1179648 | tf_op jit(solution)/shard_map/reshape;reshape | solution.py:35
  136.0 0.0 copy-start.2
  136.0 8.0 %reduce_sum.58 = f32[9,32,32]{2,1,0:T(8,128)S(1)} reduce(f32[9,32,4,32,4]{4,3,2,1,0:T(8,128)} %reshape_reshape.15, f32[]{:T(128)} %constant.38.clone.1), dimensions={2,4}, to_apply=%region_5.6 | reduce | flops 138240 | bytes 626692 | tf_op jit(solution)/shard_map/reduce_sum | solution.py:35
  144.0 0.0 copy-done
  144.0 0.0 copy-done.2
  144.0 0.2 fusion.4
  144.2 0.2 fusion.5
  144.4 0.2 fusion.6
  144.6 0.2 fusion.7
  144.9 54.3 %psum.14 = f32[256]{0:T(256)S(1)} all-reduce(f32[256]{0:T(256)S(1)} %select_add_fusion), channel_id=1, replica_groups=mesh['snap'=16,'plane'=32] {'plane'}, use_global_device_ids=true, to_apply=%region_6.7 | all-reduce | flops 256 | bytes 2048 | tf_op jit(solution)/shard_map/psum | solution.py:61
  199.1 0.7 multiply_bitcast_fusion.4
  199.8 0.0 all-reduce.10.cloned.1.call-update
  199.9 0.0 all-reduce.8.cloned.1.call-start
  199.9 1.3 dynamic-slice
  201.8 109.0 %all-reduce.10.cloned.1.call-done = f32[2,1,32,256]{3,2,1,0:T(8,128)} async-done(((f32[2,1,32,256]{3,2,1,0:T(8,128)}), f32[2,1,32,256]{3,2,1,0:T(8,128)}) %all-reduce.10.cloned.1.call-update) | async-done | bytes 65552
  310.8 0.7 constant_dynamic-slice_fusion
  311.6 0.0 copy-start.4
  311.6 1.1 convolution_bitcast_fusion.4
  312.7 0.0 all-reduce.8.cloned.1.call-update
  312.7 469.1 %all-reduce.8.cloned.1.call-done = f32[256,256]{1,0:T(8,128)} async-done(((f32[256,256]{1,0:T(8,128)}), f32[256,256]{1,0:T(8,128)}) %all-reduce.8.cloned.1.call-update) | async-done | bytes 262160 | tf_op jit(solution)/shard_map/psum | solution.py:73
  781.8 1.7 broadcast_multiply_fusion
  783.5 0.0 copy-done.4
  (7 shorter events, 0.2 us)
Async XLA Ops:
  7.2 136.9 %copy-start = (bf16[32,256]{1,0:T(8,128)(2,1)S(1)}, bf16[32,256]{1,0:T(8,128)(2,1)}, u32[]{:S(2)}) copy-start(bf16[32,256]{1,0:T(8,128)(2,1)} %param.14) | copy-start | bytes 49156
  7.2 6.3 copy-start.5
  7.2 12.0 %copy-start.3 = (f32[3,2,3,3]{3,1,2,0:T(2,128)S(1)}, f32[3,2,3,3]{3,1,2,0:T(2,128)}, u32[]{:S(2)}) copy-start(f32[3,2,3,3]{3,1,2,0:T(2,128)} %param.11) | copy-start | bytes 652
  7.2 12.3 %copy-start.7 = (bf16[1,2,4,128]{3,2,1,0:T(4,128)(2,1)S(1)}, bf16[1,2,4,128]{3,2,1,0:T(4,128)(2,1)}, u32[]{:S(2)}) copy-start(bf16[1,2,4,128]{3,2,1,0:T(4,128)(2,1)} %param.15) | copy-start | bytes 6148
  7.2 303.6 %all-reduce.10.cloned.1.call-start = ((), (), s32[]{:S(2)}) async-start(), calls=%async_computation.1 | async-start | bytes 131072
  9.1 16.5 %collective-permute-start = (bf16[1,3,128,128]{3,2,1,0:T(8,128)(2,1)S(1)}, bf16[1,3,128,128]{3,2,1,0:T(8,128)(2,1)S(1)}, u32[]{:S(2)}, u32[]{:S(2)}) collective-permute-start(bf16[1,3,128,128]{3,2,1,0:T(8,128)(2,1)S(1)} %get-tuple-element.29), channel_id=1, source_target_pairs={{1,0},{2,1},{3,2},{4,3},{5,4},{6,5},{7,6},{8,7},{9,8},{10,9},{11,1... | collective-permute-start | bytes 294920 | tf_op jit(solution)/shard_map/ppermute | solution.py:13
  10.4 15.2 %collective-permute-start.1 = (bf16[1,3,128,128]{3,2,1,0:T(8,128)(2,1)S(1)}, bf16[1,3,128,128]{3,2,1,0:T(8,128)(2,1)S(1)}, u32[]{:S(2)}, u32[]{:S(2)}) collective-permute-start(bf16[1,3,128,128]{3,2,1,0:T(8,128)(2,1)S(1)} %get-tuple-element.28), channel_id=1, source_target_pairs={{0,1},{1,2},{2,3},{3,4},{4,5},{5,6},{6,7},{7,8},{8,9},{9,10},{10,1... | collective-permute-start | bytes 294920 | tf_op jit(solution)/shard_map/ppermute | solution.py:13
  23.6 1.4 copy-start.6
  23.6 2.0 copy-start.1
  136.0 8.0 %copy-start.2 = (bf16[8,9,32,256]{3,2,1,0:T(8,128)(2,1)S(1)}, bf16[8,9,32,256]{3,2,1,0:T(8,128)(2,1)}, u32[]{:S(2)}) copy-start(bf16[8,9,32,256]{3,2,1,0:T(8,128)(2,1)} %param.13) | copy-start | bytes 3538948
  199.9 582.0 %all-reduce.8.cloned.1.call-start = ((), (), s32[]{:S(2)}) async-start(), calls=%async_computation | async-start | bytes 524288 | tf_op jit(solution)/shard_map/psum | solution.py:73
  311.6 471.9 %copy-start.4 = (f32[2,1,2,256]{3,2,1,0:T(2,128)}, f32[2,1,2,256]{3,2,1,0:T(2,128)S(1)}, u32[]{:S(2)}) copy-start(f32[2,1,2,256]{3,2,1,0:T(2,128)S(1)} %constant_dynamic-slice_fusion) | copy-start | bytes 12292
Sparse Core Ops, SparseCore 0:
  200.0 110.8 all-reduce.9
  316.9 464.9 all-reduce.7
where the time goes:
time: 791 us; the launch traced here: 790 us
  waiting for transfers between devices  578 us (73%)
  local copies, waits for them, and re-layouts  87.4 us (11%)
  blocking collectives  54.3 us (7%)
  other arithmetic  40.9 us (5%)
  between operations  23.3 us (3%)
    psum x1, waiting for transfers between devices, per_device(): gram = lax.psum(local_gram, ('snap', 'plane')) / jnp.float32(total_rows)  469 us
    unnamed x3, waiting for transfers between devices  109 us
    another operation x4, local copies, waits for them, and re-layouts, features(): filtered = grads.reshape(snaps, 9, zw // 4, 4, xw // 4, 4).mean(axis=(3, 5))  83.6 us
    psum x1, blocking collectives, per_device(): coef = lax.psum(coef, 'plane')  54.3 us
    reduce_sum x4, other arithmetic, features(): filtered = grads.reshape(snaps, 9, zw // 4, 4, xw // 4, 4).mean(axis=(3, 5))  31.8 us
  transfers between devices with their start and end apart: 4, of which 2 were waited for; matrix products, arithmetic and copies ran while one was open for 1% of the time, Pallas kernels for 0%

commit v1 on v0

--- a/solution.py
+++ b/solution.py
@@ -70,7 +70,10 @@
     total_rows = 2 * (X // 4) * (ZW // 4)
     flat = sketch.reshape(-1, sketch.shape[-1])
     local_gram = jnp.dot(flat.T, flat, precision=lax.Precision.HIGHEST)
-    gram = lax.psum(local_gram, ("snap", "plane")) / jnp.float32(total_rows)
+    obtain_limits_over_axis = lambda values: lax.psum(
+        lax.psum(values, axis_name="snap"), axis_name="plane"
+    )
+    gram = obtain_limits_over_axis(local_gram) / jnp.float32(total_rows)
     return (sketch, gram)
 
 

time: 791 us -> 652 us (0.82)
  the two profiles are of different devices: /device:TPU:2 before, /device:TPU:1 now
where the time goes in v1:
time: 652 us
  waiting for transfers between devices  441 us (68%)
  local copies, waits for them, and re-layouts  87.4 us (13%)
  blocking collectives  47 us (7%)
  other arithmetic  40.9 us (6%)
  between operations  23 us (4%)
  starting transfers between devices  10.8 us (2%)
    psum x1, waiting for transfers between devices, per_device(): lax.psum(lax.psum(values, axis_name='snap'), axis_name='plane')  214 us
    psum x1, waiting for transfers between devices, per_device(): lax.psum(values, axis_name='snap')  117 us
    unnamed x4, waiting for transfers between devices  109 us
    another operation x4, local copies, waits for them, and re-layouts, features(): filtered = grads.reshape(snaps, 9, zw // 4, 4, xw // 4, 4).mean(axis=(3, 5))  83.6 us
    psum x1, blocking collectives, per_device(): coef = lax.psum(coef, 'plane')  47 us
    reduce_sum x4, other arithmetic, features(): filtered = grads.reshape(snaps, 9, zw // 4, 4, xw // 4, 4).mean(axis=(3, 5))  31.8 us
  transfers between devices with their start and end apart: 5, of which 3 were waited for; matrix products, arithmetic and copies ran while one was open for 1% of the time, Pallas kernels for 0%

profile of v1, /device:TPU:1, one launch (start us, length us, event | category | flops | bytes accessed | tf_op | source)
XLA Modules:
  0.0 651.6 jit_solution(2219740350577038557)
XLA Ops:
  7.2 0.0 copy-start
  7.2 0.0 copy-start.5
  7.2 0.0 copy-start.3
  7.2 0.0 copy-start.7
  7.2 0.0 all-reduce.13.cloned.1.call-start
  7.9 1.2 fusion.21
  9.1 8.7 %collective-permute-start = (bf16[1,3,128,128]{3,2,1,0:T(8,128)(2,1)S(1)}, bf16[1,3,128,128]{3,2,1,0:T(8,128)(2,1)S(1)}, u32[]{:S(2)}, u32[]{:S(2)}) collective-permute-start(bf16[1,3,128,128]{3,2,1,0:T(8,128)(2,1)S(1)} %get-tuple-element.29), channel_id=1, source_target_pairs={{1,0},{2,1},{3,2},{4,3},{5,4},{6,5},{7,6},{8,7},{9,8},{10,9},{11,1... | collective-permute-start | bytes 294920 | tf_op jit(solution)/shard_map/ppermute | solution.py:13
  17.8 1.9 collective-permute-start.1
  19.8 0.0 copy-done.5
  19.8 0.7 fusion.23
  25.5 0.0 copy-done.3
  25.6 0.2 slice_reduce_fusion.17
  25.8 0.0 copy-done.7
  25.8 0.1 reduce_sum.53
  25.9 0.1 reduce_sum.54
  28.6 1.3 add_bitcast_fusion.7
  29.9 0.0 copy-start.6
  29.9 0.0 copy-start.1
  29.9 1.3 add_bitcast_fusion.6
  31.3 0.0 copy-done.6
  31.3 0.7 fusion.22
  32.0 0.0 collective-permute-done
  32.0 0.0 collective-permute-done.1
  32.0 0.0 copy-done.1
  32.0 2.7 multiply_bitcast_fusion.3
  34.6 0.1 pad_maximum_fusion
  34.8 21.0 %reshape_reshape.12 = f32[9,32,4,32,4]{4,3,2,1,0:T(8,128)} reshape(f32[1,3,3,128,128]{4,3,2,1,0:T(8,128)S(1)} %copy.14) | data formatting | bytes 1179648 | tf_op jit(solution)/shard_map/reshape;reshape | solution.py:35
  55.8 7.9 %reduce_sum.55 = f32[9,32,32]{2,1,0:T(8,128)S(1)} reduce(f32[9,32,4,32,4]{4,3,2,1,0:T(8,128)} %reshape_reshape.12, f32[]{:T(128)} %constant.38.clone.1), dimensions={2,4}, to_apply=%region_2.3 | reduce | flops 138240 | bytes 626692 | tf_op jit(solution)/shard_map/reduce_sum | solution.py:35
  63.8 20.8 %reshape_reshape.13 = f32[9,32,4,32,4]{4,3,2,1,0:T(8,128)} reshape(f32[1,3,3,128,128]{4,3,2,1,0:T(8,128)S(1)} %copy.15) | data formatting | bytes 1179648 | tf_op jit(solution)/shard_map/reshape;reshape | solution.py:35
  84.6 7.9 %reduce_sum.56 = f32[9,32,32]{2,1,0:T(8,128)S(1)} reduce(f32[9,32,4,32,4]{4,3,2,1,0:T(8,128)} %reshape_reshape.13, f32[]{:T(128)} %constant.38.clone.1), dimensions={2,4}, to_apply=%region_3.4 | reduce | flops 138240 | bytes 626692 | tf_op jit(solution)/shard_map/reduce_sum | solution.py:35
  92.5 0.1 pad_maximum_fusion.2
  92.7 20.8 %reshape_reshape.14 = f32[9,32,4,32,4]{4,3,2,1,0:T(8,128)} reshape(f32[1,3,3,128,128]{4,3,2,1,0:T(8,128)S(1)} %copy.16) | data formatting | bytes 1179648 | tf_op jit(solution)/shard_map/reshape;reshape | solution.py:35
  113.5 7.9 %reduce_sum.57 = f32[9,32,32]{2,1,0:T(8,128)S(1)} reduce(f32[9,32,4,32,4]{4,3,2,1,0:T(8,128)} %reshape_reshape.14, f32[]{:T(128)} %constant.38.clone.1), dimensions={2,4}, to_apply=%region_4.5 | reduce | flops 138240 | bytes 626692 | tf_op jit(solution)/shard_map/reduce_sum | solution.py:35
  121.5 20.8 %reshape_reshape.15 = f32[9,32,4,32,4]{4,3,2,1,0:T(8,128)} reshape(f32[1,3,3,128,128]{4,3,2,1,0:T(8,128)S(1)} %copy.17) | data formatting | bytes 1179648 | tf_op jit(solution)/shard_map/reshape;reshape | solution.py:35
  142.3 0.0 copy-start.2
  142.4 8.0 %reduce_sum.58 = f32[9,32,32]{2,1,0:T(8,128)S(1)} reduce(f32[9,32,4,32,4]{4,3,2,1,0:T(8,128)} %reshape_reshape.15, f32[]{:T(128)} %constant.38.clone.1), dimensions={2,4}, to_apply=%region_5.6 | reduce | flops 138240 | bytes 626692 | tf_op jit(solution)/shard_map/reduce_sum | solution.py:35
  150.4 0.0 copy-done
  150.4 0.0 copy-done.2
  150.4 0.2 fusion.4
  150.6 0.2 fusion.5
  150.8 0.2 fusion.6
  151.0 0.2 fusion.7
  151.2 47.0 %psum.21 = f32[256]{0:T(256)S(1)} all-reduce(f32[256]{0:T(256)S(1)} %select_add_fusion), channel_id=1, replica_groups=mesh['snap'=16,'plane'=32] {'plane'}, use_global_device_ids=true, to_apply=%region_6.7 | all-reduce | flops 256 | bytes 2048 | tf_op jit(solution)/shard_map/psum | solution.py:61
  198.2 0.7 multiply_bitcast_fusion.4
  198.9 0.0 all-reduce.13.cloned.1.call-update
  198.9 0.0 all-reduce.9.cloned.1.call-start
  199.0 1.3 dynamic-slice
  200.9 109.3 %all-reduce.13.cloned.1.call-done = f32[2,1,32,256]{3,2,1,0:T(8,128)} async-done(((f32[2,1,32,256]{3,2,1,0:T(8,128)}), f32[2,1,32,256]{3,2,1,0:T(8,128)}) %all-reduce.13.cloned.1.call-update) | async-done | bytes 65552
  310.2 0.7 constant_dynamic-slice_fusion
  310.9 0.0 copy-start.4
  310.9 1.1 convolution_bitcast_fusion.4
  312.1 0.0 all-reduce.9.cloned.1.call-update
  312.1 0.0 all-reduce.11.cloned.1.call-start
  312.1 116.8 %all-reduce.9.cloned.1.call-done = f32[256,256]{1,0:T(8,128)} async-done(((f32[256,256]{1,0:T(8,128)}), f32[256,256]{1,0:T(8,128)}) %all-reduce.9.cloned.1.call-update) | async-done | bytes 262160 | tf_op jit(solution)/shard_map/psum | solution.py:74
  429.0 0.0 all-reduce.11.cloned.1.call-update
  429.0 214.4 %all-reduce.11.cloned.1.call-done = f32[256,256]{1,0:T(8,128)} async-done(((f32[256,256]{1,0:T(8,128)}), f32[256,256]{1,0:T(8,128)}) %all-reduce.11.cloned.1.call-update) | async-done | bytes 262160 | tf_op jit(solution)/shard_map/psum | solution.py:73
  643.4 1.7 broadcast_multiply_fusion
  645.0 0.0 copy-done.4
  (7 shorter events, 0.2 us)
Async XLA Ops:
  7.2 143.2 %copy-start = (bf16[32,256]{1,0:T(8,128)(2,1)S(1)}, bf16[32,256]{1,0:T(8,128)(2,1)}, u32[]{:S(2)}) copy-start(bf16[32,256]{1,0:T(8,128)(2,1)} %param.14) | copy-start | bytes 49156
  7.2 12.6 %copy-start.5 = (s32[1,4]{1,0:T(1,128)S(1)}, s32[1,4]{1,0:T(1,128)}, u32[]{:S(2)}) copy-start(s32[1,4]{1,0:T(1,128)} %param.12) | copy-start | bytes 52
  7.2 18.4 %copy-start.3 = (f32[3,2,3,3]{3,1,2,0:T(2,128)S(1)}, f32[3,2,3,3]{3,1,2,0:T(2,128)}, u32[]{:S(2)}) copy-start(f32[3,2,3,3]{3,1,2,0:T(2,128)} %param.11) | copy-start | bytes 652
  7.2 18.6 %copy-start.7 = (bf16[1,2,4,128]{3,2,1,0:T(4,128)(2,1)S(1)}, bf16[1,2,4,128]{3,2,1,0:T(4,128)(2,1)}, u32[]{:S(2)}) copy-start(bf16[1,2,4,128]{3,2,1,0:T(4,128)(2,1)} %param.15) | copy-start | bytes 6148
  7.2 303.0 %all-reduce.13.cloned.1.call-start = ((), (), s32[]{:S(2)}) async-start(), calls=%async_computation.2 | async-start | bytes 131072
  9.1 22.9 %collective-permute-start = (bf16[1,3,128,128]{3,2,1,0:T(8,128)(2,1)S(1)}, bf16[1,3,128,128]{3,2,1,0:T(8,128)(2,1)S(1)}, u32[]{:S(2)}, u32[]{:S(2)}) collective-permute-start(bf16[1,3,128,128]{3,2,1,0:T(8,128)(2,1)S(1)} %get-tuple-element.29), channel_id=1, source_target_pairs={{1,0},{2,1},{3,2},{4,3},{5,4},{6,5},{7,6},{8,7},{9,8},{10,9},{11,1... | collective-permute-start | bytes 294920 | tf_op jit(solution)/shard_map/ppermute | solution.py:13
  17.8 14.1 %collective-permute-start.1 = (bf16[1,3,128,128]{3,2,1,0:T(8,128)(2,1)S(1)}, bf16[1,3,128,128]{3,2,1,0:T(8,128)(2,1)S(1)}, u32[]{:S(2)}, u32[]{:S(2)}) collective-permute-start(bf16[1,3,128,128]{3,2,1,0:T(8,128)(2,1)S(1)} %get-tuple-element.28), channel_id=1, source_target_pairs={{0,1},{1,2},{2,3},{3,4},{4,5},{5,6},{6,7},{7,8},{8,9},{9,10},{10,1... | collective-permute-start | bytes 294920 | tf_op jit(solution)/shard_map/ppermute | solution.py:13
  29.9 1.4 copy-start.6
  29.9 2.0 copy-start.1
  142.3 8.0 %copy-start.2 = (bf16[8,9,32,256]{3,2,1,0:T(8,128)(2,1)S(1)}, bf16[8,9,32,256]{3,2,1,0:T(8,128)(2,1)}, u32[]{:S(2)}) copy-start(bf16[8,9,32,256]{3,2,1,0:T(8,128)(2,1)} %param.13) | copy-start | bytes 3538948
  198.9 230.1 %all-reduce.9.cloned.1.call-start = ((), (), s32[]{:S(2)}) async-start(), calls=%async_computation | async-start | bytes 524288 | tf_op jit(solution)/shard_map/psum | solution.py:74
  310.9 334.1 %copy-start.4 = (f32[2,1,2,256]{3,2,1,0:T(2,128)}, f32[2,1,2,256]{3,2,1,0:T(2,128)S(1)}, u32[]{:S(2)}) copy-start(f32[2,1,2,256]{3,2,1,0:T(2,128)S(1)} %constant_dynamic-slice_fusion) | copy-start | bytes 12292
  312.1 331.3 %all-reduce.11.cloned.1.call-start = ((), (), s32[]{:S(2)}) async-start(), calls=%async_computation.1 | async-start | bytes 524288 | tf_op jit(solution)/shard_map/psum | solution.py:73
Sparse Core Ops, SparseCore 0:
  199.0 111.1 all-reduce.12
  313.9 114.9 all-reduce.8
  431.3 212.0 all-reduce.10
